TPU v7x, 32 devices: a whole 2x2x4 slice. The times are simulated.
32 devices in a mesh: row: 4 (over x, core), col: 8 (over z, y).
Axes of the slice: x: 2, y: 2, z: 4, core: 2. Of those that a mesh axis runs over, the one named last changes fastest.
Arguments:
- masters: float32 [128, 4096], P('col'), may hold values from -6 to 6
- inst_master: int32 [64, 128], P('row', 'col'), may hold values from 0 to 127
- inst_orient: int32 [64, 128], P('row', 'col'), may hold values from 0 to 3
- owner_map: int32 [128], replicated, may hold values from 0 to 127, each once
- tile_free: float32 [4096, 8192], P('row', 'col'), may hold values from -3 to 3
- target: float32 [4096, 8192], P('row', 'col'), may hold values from 0 to 1
- kernel_spectra: float32 [2, 128, 8, 128], replicated, may hold values from -6 to 6
- socs_weights: float32 [8], replicated, may hold values from 0.05 to 1
Outputs:
- resist: float32 [4096, 8192], P('row', 'col')
- new_mask: float32 [4096, 8192], P('row', 'col')
- masters_out: float32 [128, 4096], P('col')
Inputs may be any that keep to these rules, and one draw needn't show every extreme that they name: `inst_orient`: bit 0 reverses a cell's rows, bit 1 its columns. `owner_map`: each storage row is used by exactly one master; storage row r lies on index r // 16 of col.
All inputs are finite; a program needn't handle non-finite values.
Results may differ from a plain program's by a relative error of at most 0.0092.
Values may be sent and summed in bfloat16 or wider, within the bound.
A program may use at most 128 MiB of HBM per device.

v0:
```python
import math
import jax
import jax.numpy as jnp
from jax import lax
from jax.sharding import PartitionSpec as P

TILE = 512
TPD = 2
HALO = 64
CELL = 64
step_free = 1.0
step_master = 0.05
resist_gain = 2.0
resist_level = 1.8


def padded_2(value, sides, width):
    for axis, dim in sides:
        peers, length = (lax.axis_size(axis), value.shape[dim])
        up = [(i, (i + 1) % peers) for i in range(peers - 1)]
        down = [(j, i) for i, j in up]
        last = lax.slice_in_dim(value, length - width, length, axis=dim)
        initial = lax.slice_in_dim(value, 0, width, axis=dim)
        before = lax.ppermute(last, axis, up)
        after = lax.ppermute(initial, axis, down)
        value = jnp.concatenate([before, value, after], axis=dim)
    return value


def dot_plain(left, right):
    return jnp.dot(left, right, preferred_element_type=jnp.float32)


def dot_right_t(left, right):
    return lax.dot_general(
        left, right, (((1,), (1,)), ((), ())), preferred_element_type=jnp.float32
    )


def dot_left_t(left, right):
    return lax.dot_general(
        left, right, (((0,), (0,)), ((), ())), preferred_element_type=jnp.float32
    )


def tables(pad_side, band_side):
    freqs = jnp.arange(band_side, dtype=jnp.int32) - band_side // 2
    pixels = jnp.arange(pad_side, dtype=jnp.int32)
    phases = freqs[:, None] * pixels[None, :] % pad_side
    angles = phases.astype(jnp.float32) * (2.0 * math.pi / pad_side)
    return (jnp.cos(angles).astype(jnp.bfloat16), jnp.sin(angles).astype(jnp.bfloat16))


def tile_step(padded, target, spectra, weights, halo_side):
    pad_side = padded.shape[0]
    band_side = spectra.shape[1]
    kernels = spectra.shape[2]
    tile_side = pad_side - 2 * halo_side
    cos_full, sin_full = tables(pad_side, band_side)
    cos_in = cos_full[:, halo_side : halo_side + tile_side]
    sin_in = sin_full[:, halo_side : halo_side + tile_side]
    forw_re = dot_plain(cos_full, padded).astype(jnp.bfloat16)
    forw_im = (-dot_plain(sin_full, padded)).astype(jnp.bfloat16)
    spec_re = (dot_right_t(forw_re, cos_full) - dot_right_t(forw_im, sin_full)) / pad_side
    spec_im = (-dot_right_t(forw_re, sin_full) - dot_right_t(forw_im, cos_full)) / pad_side
    kern_re = spectra[0]
    kern_im = spectra[1]
    amp_re = (kern_re * spec_re[:, None, :] - kern_im * spec_im[:, None, :]).astype(jnp.bfloat16)
    amp_im = (kern_re * spec_im[:, None, :] + kern_im * spec_re[:, None, :]).astype(jnp.bfloat16)
    amp_re = amp_re.reshape(band_side, kernels * band_side)
    amp_im = amp_im.reshape(band_side, kernels * band_side)
    half_re = (dot_left_t(cos_in, amp_re) - dot_left_t(sin_in, amp_im)).astype(jnp.bfloat16)
    half_im = (dot_left_t(cos_in, amp_im) + dot_left_t(sin_in, amp_re)).astype(jnp.bfloat16)
    half_re = half_re.reshape(tile_side * kernels, band_side)
    half_im = half_im.reshape(tile_side * kernels, band_side)
    field_re = (dot_plain(half_re, cos_in) - dot_plain(half_im, sin_in)) / band_side
    field_im = (dot_plain(half_re, sin_in) + dot_plain(half_im, cos_in)) / band_side
    field_re = field_re.reshape(tile_side, kernels, tile_side)
    field_im = field_im.reshape(tile_side, kernels, tile_side)
    scaled = weights[None, :, None]
    intensity = jnp.sum(scaled * (field_re * field_re + field_im * field_im), axis=1)
    resist = jax.nn.sigmoid(resist_gain * (intensity - resist_level))
    slopes = 2.0 * (resist - target) * resist_gain * resist * (1.0 - resist)
    back_re = (2.0 / band_side * scaled * slopes[:, None, :] * field_re).astype(jnp.bfloat16)
    back_im = (2.0 / band_side * scaled * slopes[:, None, :] * field_im).astype(jnp.bfloat16)
    back_re = back_re.reshape(tile_side * kernels, tile_side)
    back_im = back_im.reshape(tile_side * kernels, tile_side)
    bhalf_re = (dot_right_t(back_re, cos_in) + dot_right_t(back_im, sin_in)).astype(jnp.bfloat16)
    bhalf_im = (dot_right_t(back_im, cos_in) - dot_right_t(back_re, sin_in)).astype(jnp.bfloat16)
    bhalf_re = bhalf_re.reshape(tile_side, kernels * band_side)
    bhalf_im = bhalf_im.reshape(tile_side, kernels * band_side)
    bamp_re = (dot_plain(cos_in, bhalf_re) + dot_plain(sin_in, bhalf_im)).reshape(
        band_side, kernels, band_side
    )
    bamp_im = (dot_plain(cos_in, bhalf_im) - dot_plain(sin_in, bhalf_re)).reshape(
        band_side, kernels, band_side
    )
    bspec_re = (jnp.sum(kern_re * bamp_re + kern_im * bamp_im, axis=1) / pad_side).astype(
        jnp.bfloat16
    )
    bspec_im = (jnp.sum(kern_re * bamp_im - kern_im * bamp_re, axis=1) / pad_side).astype(
        jnp.bfloat16
    )
    bforw_re = (dot_plain(bspec_re, cos_in) - dot_plain(bspec_im, sin_in)).astype(jnp.bfloat16)
    bforw_im = (-dot_plain(bspec_re, sin_in) - dot_plain(bspec_im, cos_in)).astype(jnp.bfloat16)
    gradient = dot_left_t(cos_in, bforw_re) - dot_left_t(sin_in, bforw_im)
    return (resist, gradient)


def orient_cells(cells, orient):
    flip_first = orient % 2 == 1
    flip_second = orient // 2 == 1
    cells = jnp.where(flip_first[..., None, None], cells[..., ::-1, :], cells)
    cells = jnp.where(flip_second[..., None, None], cells[..., :, ::-1], cells)
    return cells


def assemble(master_rows, slots, orient, cell_side):
    grid_rows, grid_cols = slots.shape
    cells = jnp.take(master_rows, slots.reshape(-1), axis=0)
    cells = cells.reshape(grid_rows, grid_cols, cell_side, cell_side)
    cells = orient_cells(cells, orient)
    return cells.transpose(0, 2, 1, 3).reshape(grid_rows * cell_side, grid_cols * cell_side)


def cells_of(image, orient, cell_side):
    grid_rows, grid_cols = orient.shape
    cells = image.reshape(grid_rows, cell_side, grid_cols, cell_side).transpose(0, 2, 1, 3)
    cells = orient_cells(cells, orient)
    return cells.reshape(grid_rows * grid_cols, cell_side * cell_side)


def smooth(master_rows, cell_side):
    grids = master_rows.reshape(-1, cell_side, cell_side)
    framed = jnp.pad(grids, ((0, 0), (1, 1), (1, 1)))
    beside_all = (
        framed[:, 2:, 1:-1] + framed[:, :-2, 1:-1] + framed[:, 1:-1, 2:] + framed[:, 1:-1, :-2]
    )
    return (0.5 * grids + 0.125 * beside_all).reshape(master_rows.shape)


def stitch_local(tiles):
    return tiles.reshape(TPD, TPD, TILE, TILE).transpose(0, 2, 1, 3).reshape(TPD * TILE, TPD * TILE)


def per_device(
    masters, inst_master, inst_orient, owner_map, tile_free, target, kernel_spectra, socs_weights
):
    stored = masters.shape[0]
    everything = lax.all_gather(masters, "col", axis=0, tiled=True)
    total_masters = everything.shape[0]
    matches = inst_master[..., None] == jnp.arange(total_masters, dtype=jnp.int32)
    slots = jnp.sum(jnp.where(matches, owner_map, 0), axis=-1)
    flat_slots = slots.reshape(-1)
    col_index = lax.axis_index("col")
    free_field = tile_free
    pad_side = TILE + 2 * HALO
    shading = jnp.tanh(assemble(everything, slots, inst_orient, CELL) + free_field)
    mask_block = shading.astype(jnp.bfloat16)
    padded = padded_2(mask_block, (("row", 0), ("col", 1)), HALO)

    def one_tile(tile_index):
        row_at = tile_index // TPD
        col_at = tile_index % TPD
        window = lax.dynamic_slice(padded, (row_at * TILE, col_at * TILE), (pad_side, pad_side))
        goal_tile = lax.dynamic_slice(target, (row_at * TILE, col_at * TILE), (TILE, TILE))
        return tile_step(window, goal_tile, kernel_spectra, socs_weights, HALO)

    resist_tiles, grad_tiles = lax.map(one_tile, jnp.arange(TPD * TPD, dtype=jnp.int32))
    resist = stitch_local(resist_tiles)
    grad_param = stitch_local(grad_tiles) * (1.0 - shading * shading)
    free_field = free_field - step_free * grad_param
    cell_grads = cells_of(grad_param, inst_orient, CELL)
    wanted = jnp.arange(total_masters, dtype=jnp.int32)
    selector = (flat_slots[None, :] == wanted[:, None]).astype(jnp.float32)
    whole_sum = lax.psum(
        jnp.dot(
            selector,
            cell_grads,
            precision=lax.Precision.HIGHEST,
            preferred_element_type=jnp.float32,
        ).astype(jnp.bfloat16),
        "row",
    )
    summed = lax.psum_scatter(whole_sum, "col", scatter_dimension=0, tiled=True).astype(jnp.float32)
    own_rows = lax.dynamic_slice_in_dim(everything, col_index * stored, stored, 0)
    fresh = smooth(own_rows - step_master * summed, CELL)
    everything = lax.all_gather(fresh.astype(jnp.bfloat16), "col", axis=0, tiled=True).astype(
        fresh.dtype
    )
    new_mask = jnp.tanh(assemble(everything, slots, inst_orient, CELL) + free_field)
    masters_out = lax.dynamic_slice_in_dim(everything, col_index * stored, stored, 0)
    return (resist, new_mask, masters_out)


def solution(mesh):
    in_specs = (
        P("col", None),
        P("row", "col"),
        P("row", "col"),
        P(),
        P("row", "col"),
        P("row", "col"),
        P(),
        P(),
    )
    out_specs = (P("row", "col"), P("row", "col"), P("col", None))
    return jax.shard_map(
        per_device, mesh=mesh, in_specs=in_specs, out_specs=out_specs, check_vma=False
    )
```

profile of v0, /device:TPU:0, one launch (start us, length us, event | category | flops | bytes accessed | tf_op | source)
XLA Modules:
  0.0 786.2 jit_solution(12624637121962711433)
XLA Ops:
  10.0 52.0 %all-gather.3.cloned.1.call-done = f32[128,4096]{1,0:T(8,128)} async-done(((f32[16,4096]{1,0:T(8,128)}), f32[128,4096]{1,0:T(8,128)}) %all-gather.3.cloned.1.call-update) | async-done | bytes 2097168 | tf_op jit(solution)/shard_map/all_gather | solution.py:150
  61.9 7.3 gather_fusion
  69.2 4.8 broadcast_select_fusion.5
  74.0 8.1 %reshape.201 = f32[16,16,64,64]{3,2,1,0:T(8,128)} reshape(f32[256,4096]{1,0:T(8,128)} %broadcast_select_fusion.5) | data formatting | bytes 8388608 | tf_op jit(solution)/shard_map/reshape | solution.py:121
  82.1 12.0 %rev.18 = f32[16,16,64,64]{3,2,1,0:T(8,128)} reverse(f32[16,16,64,64]{3,2,1,0:T(8,128)} %reshape.201), dimensions={2} | reverse | bytes 8388608 | tf_op jit(solution)/shard_map/rev | solution.py:113
  94.1 9.8 %broadcast_select_fusion.2 = f32[16,16,64,64]{3,2,1,0:T(8,128)} fusion(f32[16,16,64,64]{3,2,1,0:T(8,128)} %rev.18, f32[16,16,64,64]{3,2,1,0:T(8,128)} %reshape.201, pred[16,16]{1,0:T(8,128)(4,1)S(1)} %get-tuple-element.182), kind=kLoop, calls=%fused_computation.136 | loop fusion | flops 1048576 | bytes 12583168 | tf_op jit(solution)/shard_map/jit(_where)/select_n | solution.py:113
  103.9 13.2 %rev.19 = f32[16,16,64,64]{3,2,1,0:T(8,128)} reverse(f32[16,16,64,64]{3,2,1,0:T(8,128)} %broadcast_select_fusion.2), dimensions={3} | reverse | bytes 8388608 | tf_op jit(solution)/shard_map/rev | solution.py:114
  117.1 6.3 select_bitcast_fusion.1
  123.4 9.8 %copy.21 = f32[16,64,16,64]{3,2,1,0:T(8,128)} copy(f32[16,64,16,64]{3,1,2,0:T(8,128)S(1)} %select_bitcast_fusion.1) | data formatting | bytes 8388608 | tf_op jit(solution)/shard_map/transpose | solution.py:123
  133.2 7.6 reshape.202
  140.8 4.6 fusion.96
  156.4 4.6 collective-permute-done.2
  161.0 5.4 collective-permute-done.3
  166.4 5.4 concatenate.7
  171.8 290.4 %while.15 = (s32[]{:T(128)}, f32[4,512,512]{2,1,0:T(8,128)}, f32[4,512,512]{2,1,0:T(8,128)}, f32[8]{0:T(128)S(1)}, f32[2,128,8,128]{3,2,1,0:T(8,128)S(1)}, /*ind...) while((s32[]{:T(128)}, f32[4,512,512]{2,1,0:T(8,128)}, ...), condition=%wide.region_5.7_spmd, body=%wide.region_1.6_spmd.sunk | while | flops 5924732928 | bytes 203478224 | solution.py:169
  206.6 4.6 fusion.246
  212.7 4.7 subtract_multiply_fusion.5
  220.7 6.5 fusion.249
  230.3 4.3 fusion.250
  234.6 4.7 fusion.251
  240.9 4.3 fusion.253
  245.2 4.7 fusion.254
  274.8 4.6 fusion.246
  281.0 4.7 subtract_multiply_fusion.5
  288.9 6.5 fusion.249
  298.5 4.3 fusion.250
  302.8 4.7 fusion.251
  309.2 4.3 fusion.253
  313.5 4.7 fusion.254
  343.0 4.6 fusion.246
  349.2 4.7 subtract_multiply_fusion.5
  357.1 6.5 fusion.249
  366.7 4.3 fusion.250
  371.0 4.7 fusion.251
  377.4 4.3 fusion.253
  381.7 4.7 fusion.254
  411.3 4.6 fusion.246
  417.4 4.7 subtract_multiply_fusion.5
  425.4 6.5 fusion.249
  435.0 4.3 fusion.250
  439.3 4.7 fusion.251
  449.9 4.7 fusion.254
  462.2 5.4 copy.23
  474.6 7.3 reshape.207
  481.9 9.2 %copy.45 = f32[16,64,16,64]{3,1,2,0:T(8,128)} copy(f32[16,64,16,64]{3,2,1,0:T(8,128)} %reshape.207) | data formatting | bytes 8388608 | tf_op jit(solution)/shard_map/reshape | solution.py:128
  491.1 11.9 %rev.20 = f32[16,16,64,64]{3,2,1,0:T(8,128)} reverse(f32[16,16,64,64]{3,2,1,0:T(8,128)} %bitcast.205), dimensions={2} | reverse | bytes 8388608 | tf_op jit(solution)/shard_map/rev | solution.py:113
  503.1 11.0 %broadcast_select_fusion.1 = f32[16,16,64,64]{3,2,1,0:T(8,128)} fusion(f32[16,16,64,64]{3,2,1,0:T(8,128)} %rev.20, pred[16,16]{1,0:T(8,128)(4,1)S(1)} %copy-done.8, f32[16,64,16,64]{3,2,1,0:T(8,128)} %reshape.207), kind=kLoop, calls=%fused_computation.135 | loop fusion | flops 1048576 | bytes 12583168 | tf_op jit(solution)/shard_map/jit(_where)/select_n | solution.py:113
  514.0 13.2 %rev.21 = f32[16,16,64,64]{3,2,1,0:T(8,128)} reverse(f32[16,16,64,64]{3,2,1,0:T(8,128)} %broadcast_select_fusion.1), dimensions={3} | reverse | bytes 8388608 | tf_op jit(solution)/shard_map/rev | solution.py:114
  527.2 9.8 %broadcast_select_fusion.3 = f32[16,16,64,64]{3,2,1,0:T(8,128)} fusion(f32[16,16,64,64]{3,2,1,0:T(8,128)} %rev.21, f32[16,16,64,64]{3,2,1,0:T(8,128)} %broadcast_select_fusion.1, pred[16,16]{1,0:T(8,128)(4,1)S(1)} %copy-done.6), kind=kLoop, calls=%fused_computation.137 | loop fusion | flops 1048576 | bytes 12583168 | tf_op jit(solution)/shard_map/jit(_where)/select_n | solution.py:114
  537.1 7.9 %reshape.208 = f32[256,4096]{1,0:T(8,128)} reshape(f32[16,16,64,64]{3,2,1,0:T(8,128)} %broadcast_select_fusion.3) | data formatting | bytes 8388608 | tf_op jit(solution)/shard_map/reshape | solution.py:130
  545.0 4.9 convolution_convert_fusion.1
  549.9 67.1 %reduce-scatter.2.cloned.1.call-done = bf16[16,4096]{1,0:T(8,128)(2,1)} async-done(((bf16[128,4096]{1,0:T(8,128)(2,1)}), bf16[16,4096]{1,0:T(8,128)(2,1)}) %reduce-scatter.2.cloned.1.call-update) | async-done | bytes 131088 | tf_op jit(solution)/shard_map/reduce_scatter | solution.py:185
  617.1 33.0 %all-reduce.3.cloned.1.call-done = bf16[16,4096]{1,0:T(8,128)(2,1)} async-done(((bf16[16,4096]{1,0:T(8,128)(2,1)}), bf16[16,4096]{1,0:T(8,128)(2,1)}) %all-reduce.3.cloned.1.call-update) | async-done | bytes 131088 | tf_op jit(solution)/shard_map/psum | solution.py:176
  652.7 5.4 copy.22
  661.1 32.0 %all-gather.5.cloned.1.call-done = bf16[128,4096]{1,0:T(8,128)(2,1)} async-done(((bf16[16,4096]{1,0:T(8,128)(2,1)}), bf16[128,4096]{1,0:T(8,128)(2,1)}) %all-gather.5.cloned.1.call-update) | async-done | bytes 1048592 | tf_op jit(solution)/shard_map/all_gather | solution.py:188
  699.3 4.8 broadcast_select_fusion.4
  704.1 8.1 %reshape.210 = f32[16,16,64,64]{3,2,1,0:T(8,128)} reshape(f32[256,4096]{1,0:T(8,128)} %broadcast_select_fusion.4) | data formatting | bytes 8388608 | tf_op jit(solution)/shard_map/reshape | solution.py:121
  712.2 12.0 %rev.22 = f32[16,16,64,64]{3,2,1,0:T(8,128)} reverse(f32[16,16,64,64]{3,2,1,0:T(8,128)} %reshape.210), dimensions={2} | reverse | bytes 8388608 | tf_op jit(solution)/shard_map/rev | solution.py:113
  724.1 9.8 %broadcast_select_fusion = f32[16,16,64,64]{3,2,1,0:T(8,128)} fusion(f32[16,16,64,64]{3,2,1,0:T(8,128)} %rev.22, f32[16,16,64,64]{3,2,1,0:T(8,128)} %reshape.210, pred[16,16]{1,0:T(8,128)(4,1)S(1)} %copy-done.8), kind=kLoop, calls=%fused_computation.134 | loop fusion | flops 1048576 | bytes 12583168 | tf_op jit(solution)/shard_map/jit(_where)/select_n | solution.py:113
  733.9 13.2 %rev.23 = f32[16,16,64,64]{3,2,1,0:T(8,128)} reverse(f32[16,16,64,64]{3,2,1,0:T(8,128)} %broadcast_select_fusion), dimensions={3} | reverse | bytes 8388608 | tf_op jit(solution)/shard_map/rev | solution.py:114
  747.1 6.3 select_bitcast_fusion
  753.5 9.8 %copy.25 = f32[16,64,16,64]{3,2,1,0:T(8,128)} copy(f32[16,64,16,64]{3,1,2,0:T(8,128)S(1)} %select_bitcast_fusion) | data formatting | bytes 8388608 | tf_op jit(solution)/shard_map/transpose | solution.py:123
  763.3 7.6 reshape.211
  770.9 8.6 %add_tanh_fusion = f32[1024,1024]{1,0:T(8,128)} fusion(f32[1024,1024]{1,0:T(8,128)} %reshape.211, f32[1024,1024]{1,0:T(8,128)} %param.16, f32[1024,1024]{1,0:T(8,128)} %subtract_multiply_fusion.2), kind=kLoop, calls=%fused_computation.131 | loop fusion | flops 2097152 | bytes 16777216 | tf_op jit(solution)/shard_map/tanh | solution.py:191
  (231 shorter events, 164.5 us)
Async XLA Ops:
  7.2 54.8 %all-gather.3.cloned.1.call-start = ((), (), s32[]{:S(2)}) async-start(), calls=%async_computation.1 | async-start | bytes 2359296 | tf_op jit(solution)/shard_map/all_gather | solution.py:150
  7.9 609.1 %reduce-scatter.2.cloned.1.call-start = ((), (), s32[]{:S(2)}) async-start(), calls=%async_computation.3 | async-start | bytes 1179648 | tf_op jit(solution)/shard_map/reduce_scatter | solution.py:185
  9.2 60.1 %copy-start.11 = (s32[256]{0:T(256)}, s32[256]{0:T(256)S(1)}, u32[]{:S(2)}) copy-start(s32[256]{0:T(256)S(1)} %reshape.200) | copy-start | bytes 3076
  9.2 60.0 %copy-start.10 = (s32[1024]{0:T(1024)}, s32[1024]{0:T(1024)S(1)}, u32[]{:S(2)}) copy-start(s32[1024]{0:T(1024)S(1)} %pad_clamp_fusion) | copy-start | bytes 12292
  9.2 60.0 %copy-start.13 = (pred[256]{0:T(512)(128)(4,1)}, pred[256]{0:T(512)(128)(4,1)S(1)}, u32[]{:S(2)}) copy-start(pred[256]{0:T(512)(128)(4,1)S(1)} %compare_and_fusion) | copy-start | bytes 772
  9.9 84.1 %copy-start.7 = (pred[16,16]{1,0:T(8,128)(4,1)}, pred[16,16]{1,0:T(8,128)(4,1)S(1)}, u32[]{:S(2)}) copy-start(pred[16,16]{1,0:T(8,128)(4,1)S(1)} %get-tuple-element.182) | copy-start | bytes 772
  10.0 107.1 %copy-start.5 = (pred[16,16]{1,0:T(8,128)(4,1)}, pred[16,16]{1,0:T(8,128)(4,1)S(1)}, u32[]{:S(2)}) copy-start(pred[16,16]{1,0:T(8,128)(4,1)S(1)} %get-tuple-element.181) | copy-start | bytes 772
  145.4 4.3 collective-permute-start.1
  146.7 4.0 collective-permute-start
  150.9 20.9 %copy-start.1 = (f32[2,128,8,128]{3,2,1,0:T(8,128)S(1)}, f32[2,128,8,128]{3,2,1,0:T(8,128)}, u32[]{:S(2)}) copy-start(f32[2,128,8,128]{3,2,1,0:T(8,128)} %param.18) | copy-start | bytes 3145732
  150.9 20.8 %copy-start.9 = (f32[8]{0:T(128)S(1)}, f32[8]{0:T(128)}, u32[]{:S(2)}) copy-start(f32[8]{0:T(128)} %param.19) | copy-start | bytes 100
  151.9 9.1 %collective-permute-start.2 = (bf16[1152,64]{1,0:T(8,128)(2,1)}, bf16[1152,64]{1,0:T(8,128)(2,1)}, u32[]{:S(2)}, u32[]{:S(2)}) collective-permute-start(bf16[1152,64]{1,0:T(8,128)(2,1)} %get-tuple-element.178), channel_id=1, source_target_pairs={{0,1},{1,2},{2,3},{3,4},{4,5},{5,6},{6,7},{8,9},{9,10},{10,11},{11... | collective-permute-start | bytes 442376 | tf_op jit(solution)/shard_map/ppermute | solution.py:24
  155.1 11.3 %collective-permute-start.3 = (bf16[1152,64]{1,0:T(8,128)(2,1)}, bf16[1152,64]{1,0:T(8,128)(2,1)}, u32[]{:S(2)}, u32[]{:S(2)}) collective-permute-start(bf16[1152,64]{1,0:T(8,128)(2,1)} %get-tuple-element.177), channel_id=1, source_target_pairs={{1,0},{2,1},{3,2},{4,3},{5,4},{6,5},{7,6},{9,8},{10,9},{11,10},{12... | collective-permute-start | bytes 442376 | tf_op jit(solution)/shard_map/ppermute | solution.py:25
  217.4 3.2 copy-start
  252.7 4.5 copy-start.2
  285.7 3.2 copy-start
  320.9 4.5 copy-start.2
  353.9 3.2 copy-start
  389.1 4.5 copy-start.2
  422.1 3.2 copy-start
  457.4 4.5 copy-start.2
  467.7 2.2 copy-start.3
  467.7 3.5 copy-start.4
  491.1 12.0 %copy-start.8 = (pred[16,16]{1,0:T(8,128)(4,1)S(1)}, pred[16,16]{1,0:T(8,128)(4,1)}, u32[]{:S(2)}) copy-start(pred[16,16]{1,0:T(8,128)(4,1)} %copy-done.7) | copy-start | bytes 772
  514.0 13.2 %copy-start.6 = (pred[16,16]{1,0:T(8,128)(4,1)S(1)}, pred[16,16]{1,0:T(8,128)(4,1)}, u32[]{:S(2)}) copy-start(pred[16,16]{1,0:T(8,128)(4,1)} %copy-done.5) | copy-start | bytes 772
  537.1 7.9 %copy-start.12 = (s32[256]{0:T(256)S(1)}, s32[256]{0:T(256)}, u32[]{:S(2)}) copy-start(s32[256]{0:T(256)} %copy-done.11) | copy-start | bytes 3076
  549.9 100.2 %all-reduce.3.cloned.1.call-start = ((), (), s32[]{:S(2)}) async-start(), calls=%async_computation.4 | async-start | bytes 262144 | tf_op jit(solution)/shard_map/psum | solution.py:176
  617.0 76.1 %all-gather.5.cloned.1.call-start = ((), (), s32[]{:S(2)}) async-start(), calls=%async_computation.2 | async-start | bytes 1179648 | tf_op jit(solution)/shard_map/all_gather | solution.py:188
  694.5 4.8 copy-start.14
Sparse Core Ops, SparseCore 0:
  10.1 51.7 all-gather.2
  550.0 66.9 reduce-scatter.1
  619.3 30.7 all-reduce.2
  652.8 40.2 all-gather.4
where the time goes:
time: 795 us; the launch traced here: 786 us
  matrix products  221 us (28%)
  local copies, waits for them, and re-layouts  208 us (26%)
  waiting for transfers between devices  196 us (25%)
  other arithmetic  111 us (14%)
  loops' own time  27.4 us (3%)
  between operations  14.3 us (2%)
  starting transfers between devices  8.95 us (1%)
    dot_general x48, matrix products, dot_plain(): return jnp.dot(left, right, preferred_element_type=jnp.float32)  105 us
    dot_general x32, matrix products, dot_right_t(): lax.dot_general(left, right, (((1,), (1,)), ((), ())), preferred_element_...  95 us
    reduce_scatter x1, waiting for transfers between devices, per_device(): lax.psum_scatter(whole_sum, 'col', scatter_dimension=0, tiled=True)  67.1 us
    all_gather x1, waiting for transfers between devices, per_device(): everything = lax.all_gather(masters, 'col', axis=0, tiled=True)  52 us
    rev x3, local copies, waits for them, and re-layouts, orient_cells(): cells = jnp.where(flip_second[..., None, None], cells[..., :, ::-1], cells)  39.6 us
    rev x3, local copies, waits for them, and re-layouts, orient_cells(): cells = jnp.where(flip_first[..., None, None], cells[..., ::-1, :], cells)  35.9 us
    psum x1, waiting for transfers between devices, per_device(): lax.psum(jnp.dot(selector, cell_grads, precision=lax.Precision.HIGHEST, p...  33 us
    all_gather x1, waiting for transfers between devices, per_device(): lax.all_gather(fresh.astype(jnp.bfloat16), 'col', axis=0, tiled=True)  32 us
  transfers between devices with their start and end apart: 8, of which 7 were waited for; matrix products, arithmetic and copies ran while one was open for 1% of the time, Pallas kernels for 0%

commit v1 on v0

--- a/solution.py
+++ b/solution.py
@@ -12,6 +12,18 @@
 step_master = 0.05
 resist_gain = 2.0
 resist_level = 1.8
+
+
+def doubled_up(x, axis, dim):
+    ways, here, step = (lax.axis_size(axis), lax.axis_index(axis), x.shape[dim])
+    line, have = (x, 1)
+    while have < ways:
+        line = jnp.concatenate(
+            [line, lax.ppermute(line, axis, [(d, (d - have) % ways) for d in range(ways)])],
+            axis=dim,
+        )
+        have = 2 * have
+    return jnp.roll(line, here * step, axis=dim)
 
 
 def padded_2(value, sides, width):
@@ -147,7 +159,7 @@
     masters, inst_master, inst_orient, owner_map, tile_free, target, kernel_spectra, socs_weights
 ):
     stored = masters.shape[0]
-    everything = lax.all_gather(masters, "col", axis=0, tiled=True)
+    everything = doubled_up(masters, "col", 0)
     total_masters = everything.shape[0]
     matches = inst_master[..., None] == jnp.arange(total_masters, dtype=jnp.int32)
     slots = jnp.sum(jnp.where(matches, owner_map, 0), axis=-1)

time: 795 us -> 819 us (1.030)
  starting transfers between devices: 8.95 us -> 19.1 us
    ppermute x0 -> x3, waiting for transfers between devices: none -> 58.1 us  [doubled_up(): lax.ppermute(line, axis, [(d, (d - have) % ways) for d in range(ways)])]
    all_gather x1 -> x0, waiting for transfers between devices: 52 us -> none  [per_device(): everything = lax.all_gather(masters, 'col', axis=0, tiled=True)]
  transfers between devices with their start and end apart: 8 -> 10, of which waited for: 7 -> 8; matrix products, arithmetic and copies ran while one was open for 1% -> 2% of each run, Pallas kernels for 0% -> 0%
where the time goes in v1:
time: 819 us; the launch traced here: 812 us
  matrix products  222 us (27%)
  local copies, waits for them, and re-layouts  216 us (26%)
  waiting for transfers between devices  199 us (24%)
  other arithmetic  113 us (14%)
  loops' own time  28.9 us (4%)
  starting transfers between devices  19.1 us (2%)
  between operations  14.3 us (2%)
    dot_general x48, matrix products, dot_plain(): return jnp.dot(left, right, preferred_element_type=jnp.float32)  105 us
    dot_general x32, matrix products, dot_right_t(): lax.dot_general(left, right, (((1,), (1,)), ((), ())), preferred_element_...  95 us
    reduce_scatter x1, waiting for transfers between devices, per_device(): lax.psum_scatter(whole_sum, 'col', scatter_dimension=0, tiled=True)  63.9 us
    ppermute x3, waiting for transfers between devices, doubled_up(): lax.ppermute(line, axis, [(d, (d - have) % ways) for d in range(ways)])  58.1 us
    rev x3, local copies, waits for them, and re-layouts, orient_cells(): cells = jnp.where(flip_second[..., None, None], cells[..., :, ::-1], cells)  39.4 us
    rev x3, local copies, waits for them, and re-layouts, orient_cells(): cells = jnp.where(flip_first[..., None, None], cells[..., ::-1, :], cells)  35.7 us
    psum x1, waiting for transfers between devices, per_device(): lax.psum(jnp.dot(selector, cell_grads, precision=lax.Precision.HIGHEST, p...  32.8 us
    all_gather x1, waiting for transfers between devices, per_device(): lax.all_gather(fresh.astype(jnp.bfloat16), 'col', axis=0, tiled=True)  32 us
  transfers between devices with their start and end apart: 10, of which 8 were waited for; matrix products, arithmetic and copies ran while one was open for 2% of the time, Pallas kernels for 0%

profile of v1, /device:TPU:0, one launch (start us, length us, event | category | flops | bytes accessed | tf_op | source)
XLA Modules:
  0.0 811.6 jit_solution(13053092851475586162)
XLA Ops:
  7.2 6.1 collective-permute-start
  23.3 9.7 %collective-permute-done.1 = f32[32,4096]{1,0:T(8,128)S(1)} collective-permute-done((f32[32,4096]{1,0:T(8,128)S(1)}, f32[32,4096]{1,0:T(8,128)S(1)}, u32[]{:S(2)}, u32[]{:S(2)}) %collective-permute-start.1) | collective-permute-done | bytes 524320 | tf_op jit(solution)/shard_map/ppermute | solution.py:22
  36.2 44.5 %collective-permute-done.2 = f32[64,4096]{1,0:T(8,128)S(1)} collective-permute-done((f32[64,4096]{1,0:T(8,128)S(1)}, f32[64,4096]{1,0:T(8,128)S(1)}, u32[]{:S(2)}, u32[]{:S(2)}) %collective-permute-start.2) | collective-permute-done | bytes 1048608 | tf_op jit(solution)/shard_map/ppermute | solution.py:22
  90.8 4.8 broadcast_select_fusion.5
  95.6 8.1 reshape.201
  103.6 11.9 %rev.18 = f32[16,16,64,64]{3,2,1,0:T(8,128)} reverse(f32[16,16,64,64]{3,2,1,0:T(8,128)} %reshape.201), dimensions={2} | reverse | bytes 8388608 | tf_op jit(solution)/shard_map/rev | solution.py:125
  115.5 9.8 %broadcast_select_fusion.2 = f32[16,16,64,64]{3,2,1,0:T(8,128)} fusion(f32[16,16,64,64]{3,2,1,0:T(8,128)} %rev.18, f32[16,16,64,64]{3,2,1,0:T(8,128)} %reshape.201, pred[16,16]{1,0:T(8,128)(4,1)S(1)} %get-tuple-element.182), kind=kLoop, calls=%fused_computation.136 | loop fusion | flops 1048576 | bytes 12583168 | tf_op jit(solution)/shard_map/jit(_where)/select_n | solution.py:125
  125.3 13.1 %rev.19 = f32[16,16,64,64]{3,2,1,0:T(8,128)} reverse(f32[16,16,64,64]{3,2,1,0:T(8,128)} %broadcast_select_fusion.2), dimensions={3} | reverse | bytes 8388608 | tf_op jit(solution)/shard_map/rev | solution.py:126
  138.5 6.3 select_bitcast_fusion.1
  144.8 9.8 %copy.21 = f32[16,64,16,64]{3,2,1,0:T(8,128)} copy(f32[16,64,16,64]{3,1,2,0:T(8,128)S(1)} %select_bitcast_fusion.1) | data formatting | bytes 8388608 | tf_op jit(solution)/shard_map/transpose | solution.py:135
  154.6 7.6 reshape.202
  162.2 4.6 fusion.96
  172.5 5.1 collective-permute-start.5
  178.9 11.3 %collective-permute-done.5 = bf16[1152,64]{1,0:T(8,128)(2,1)S(1)} collective-permute-done((bf16[1152,64]{1,0:T(8,128)(2,1)S(1)}, bf16[1152,64]{1,0:T(8,128)(2,1)S(1)}, u32[]{:S(2)}, u32[]{:S(2)}) %collective-permute-start.5) | collective-permute-done | bytes 147488 | tf_op jit(solution)/shard_map/ppermute | solution.py:36
  194.2 296.6 %while.15 = (s32[]{:T(128)}, f32[4,512,512]{2,1,0:T(8,128)}, f32[4,512,512]{2,1,0:T(8,128)}, f32[8]{0:T(128)S(1)}, f32[2,128,8,128]{3,2,1,0:T(8,128)}, /*index=5...) while((s32[]{:T(128)}, f32[4,512,512]{2,1,0:T(8,128)}, ...), condition=%wide.region_5.7_spmd, body=%wide.region_1.6_spmd.sunk | while | flops 5924732928 | bytes 201381072 | solution.py:181
  230.5 4.6 fusion.246
  236.7 4.7 subtract_multiply_fusion.5
  244.6 6.6 fusion.249
  254.2 4.3 fusion.250
  258.5 4.7 fusion.251
  264.9 4.3 fusion.253
  269.2 4.7 fusion.254
  300.3 4.6 fusion.246
  306.5 4.7 subtract_multiply_fusion.5
  314.4 6.6 fusion.249
  324.0 4.3 fusion.250
  328.3 4.7 fusion.251
  334.7 4.3 fusion.253
  339.0 4.7 fusion.254
  370.1 4.6 fusion.246
  376.3 4.7 subtract_multiply_fusion.5
  384.2 6.6 fusion.249
  393.8 4.3 fusion.250
  398.1 4.7 fusion.251
  404.5 4.3 fusion.253
  408.8 4.7 fusion.254
  440.0 4.6 fusion.246
  446.1 4.7 subtract_multiply_fusion.5
  454.0 6.6 fusion.249
  463.7 4.3 fusion.250
  468.0 4.7 fusion.251
  478.6 4.7 fusion.254
  490.8 5.4 copy.23
  503.2 7.3 reshape.207
  510.5 9.2 %copy.45 = f32[16,64,16,64]{3,1,2,0:T(8,128)} copy(f32[16,64,16,64]{3,2,1,0:T(8,128)} %reshape.207) | data formatting | bytes 8388608 | tf_op jit(solution)/shard_map/reshape | solution.py:140
  519.7 11.9 %rev.20 = f32[16,16,64,64]{3,2,1,0:T(8,128)} reverse(f32[16,16,64,64]{3,2,1,0:T(8,128)} %bitcast.205), dimensions={2} | reverse | bytes 8388608 | tf_op jit(solution)/shard_map/rev | solution.py:125
  531.6 10.9 %broadcast_select_fusion.1 = f32[16,16,64,64]{3,2,1,0:T(8,128)} fusion(f32[16,16,64,64]{3,2,1,0:T(8,128)} %rev.20, pred[16,16]{1,0:T(8,128)(4,1)S(1)} %copy-done.9, f32[16,64,16,64]{3,2,1,0:T(8,128)} %reshape.207), kind=kLoop, calls=%fused_computation.135 | loop fusion | flops 1048576 | bytes 12583168 | tf_op jit(solution)/shard_map/jit(_where)/select_n | solution.py:125
  542.6 13.1 %rev.21 = f32[16,16,64,64]{3,2,1,0:T(8,128)} reverse(f32[16,16,64,64]{3,2,1,0:T(8,128)} %broadcast_select_fusion.1), dimensions={3} | reverse | bytes 8388608 | tf_op jit(solution)/shard_map/rev | solution.py:126
  555.7 9.8 %broadcast_select_fusion.3 = f32[16,16,64,64]{3,2,1,0:T(8,128)} fusion(f32[16,16,64,64]{3,2,1,0:T(8,128)} %rev.21, f32[16,16,64,64]{3,2,1,0:T(8,128)} %broadcast_select_fusion.1, pred[16,16]{1,0:T(8,128)(4,1)S(1)} %copy-done.7), kind=kLoop, calls=%fused_computation.137 | loop fusion | flops 1048576 | bytes 12583168 | tf_op jit(solution)/shard_map/jit(_where)/select_n | solution.py:126
  565.5 7.9 reshape.208
  573.4 4.9 convolution_convert_fusion.1
  578.3 63.9 %reduce-scatter.2.cloned.1.call-done = bf16[16,4096]{1,0:T(8,128)(2,1)} async-done(((bf16[128,4096]{1,0:T(8,128)(2,1)}), bf16[16,4096]{1,0:T(8,128)(2,1)}) %reduce-scatter.2.cloned.1.call-update) | async-done | bytes 131088 | tf_op jit(solution)/shard_map/reduce_scatter | solution.py:197
  642.6 32.8 %all-reduce.3.cloned.1.call-done = bf16[16,4096]{1,0:T(8,128)(2,1)} async-done(((bf16[16,4096]{1,0:T(8,128)(2,1)}), bf16[16,4096]{1,0:T(8,128)(2,1)}) %all-reduce.3.cloned.1.call-update) | async-done | bytes 131088 | tf_op jit(solution)/shard_map/psum | solution.py:188
  678.0 5.4 copy.22
  686.5 32.0 %all-gather.2.cloned.1.call-done = bf16[128,4096]{1,0:T(8,128)(2,1)} async-done(((bf16[16,4096]{1,0:T(8,128)(2,1)}), bf16[128,4096]{1,0:T(8,128)(2,1)}) %all-gather.2.cloned.1.call-update) | async-done | bytes 1048592 | tf_op jit(solution)/shard_map/all_gather | solution.py:200
  724.7 4.8 broadcast_select_fusion.4
  729.4 8.1 %reshape.210 = f32[16,16,64,64]{3,2,1,0:T(8,128)} reshape(f32[256,4096]{1,0:T(8,128)} %broadcast_select_fusion.4) | data formatting | bytes 8388608 | tf_op jit(solution)/shard_map/reshape | solution.py:133
  737.6 11.9 %rev.22 = f32[16,16,64,64]{3,2,1,0:T(8,128)} reverse(f32[16,16,64,64]{3,2,1,0:T(8,128)} %reshape.210), dimensions={2} | reverse | bytes 8388608 | tf_op jit(solution)/shard_map/rev | solution.py:125
  749.5 9.8 %broadcast_select_fusion = f32[16,16,64,64]{3,2,1,0:T(8,128)} fusion(f32[16,16,64,64]{3,2,1,0:T(8,128)} %rev.22, f32[16,16,64,64]{3,2,1,0:T(8,128)} %reshape.210, pred[16,16]{1,0:T(8,128)(4,1)S(1)} %copy-done.9), kind=kLoop, calls=%fused_computation.134 | loop fusion | flops 1048576 | bytes 12583168 | tf_op jit(solution)/shard_map/jit(_where)/select_n | solution.py:125
  759.3 13.1 %rev.23 = f32[16,16,64,64]{3,2,1,0:T(8,128)} reverse(f32[16,16,64,64]{3,2,1,0:T(8,128)} %broadcast_select_fusion), dimensions={3} | reverse | bytes 8388608 | tf_op jit(solution)/shard_map/rev | solution.py:126
  772.4 6.3 select_bitcast_fusion
  778.7 9.8 %copy.25 = f32[16,64,16,64]{3,2,1,0:T(8,128)} copy(f32[16,64,16,64]{3,1,2,0:T(8,128)S(1)} %select_bitcast_fusion) | data formatting | bytes 8388608 | tf_op jit(solution)/shard_map/transpose | solution.py:135
  788.5 7.6 reshape.211
  796.1 8.6 %add_tanh_fusion = f32[1024,1024]{1,0:T(8,128)} fusion(f32[1024,1024]{1,0:T(8,128)} %reshape.211, f32[1024,1024]{1,0:T(8,128)} %param.16, f32[1024,1024]{1,0:T(8,128)} %subtract_multiply_fusion.2), kind=kLoop, calls=%fused_computation.131 | loop fusion | flops 2097152 | bytes 16777216 | tf_op jit(solution)/shard_map/tanh | solution.py:203
  (253 shorter events, 189.9 us)
Async XLA Ops:
  7.2 74.6 %copy-start.5 = (f32[16,4096]{1,0:T(8,128)S(1)}, f32[16,4096]{1,0:T(8,128)}, u32[]{:S(2)}) copy-start(f32[16,4096]{1,0:T(8,128)} %param.12) | copy-start | bytes 786436
  7.2 635.1 %reduce-scatter.2.cloned.1.call-start = ((), (), s32[]{:S(2)}) async-start(), calls=%async_computation.2 | async-start | bytes 1179648 | tf_op jit(solution)/shard_map/reduce_scatter | solution.py:197
  7.2 12.0 %collective-permute-start = (f32[16,4096]{1,0:T(8,128)}, f32[16,4096]{1,0:T(8,128)S(1)}, u32[]{:S(2)}, u32[]{:S(2)}) collective-permute-start(f32[16,4096]{1,0:T(8,128)} %param.12), channel_id=1, source_target_pairs={{0,7},{1,0},{2,1},{3,2},{4,3},{5,4},{6,5},{7,6},{8,15},{9,8},{10,9... | collective-permute-start | bytes 786440 | tf_op jit(solution)/shard_map/ppermute | solution.py:22
  14.5 20.0 %copy-start.12 = (s32[256]{0:T(256)}, s32[256]{0:T(256)S(1)}, u32[]{:S(2)}) copy-start(s32[256]{0:T(256)S(1)} %reshape.200) | copy-start | bytes 3076
  15.3 100.3 %copy-start.8 = (pred[16,16]{1,0:T(8,128)(4,1)}, pred[16,16]{1,0:T(8,128)(4,1)S(1)}, u32[]{:S(2)}) copy-start(pred[16,16]{1,0:T(8,128)(4,1)S(1)} %get-tuple-element.182) | copy-start | bytes 772
  15.3 123.2 %copy-start.6 = (pred[16,16]{1,0:T(8,128)(4,1)}, pred[16,16]{1,0:T(8,128)(4,1)S(1)}, u32[]{:S(2)}) copy-start(pred[16,16]{1,0:T(8,128)(4,1)S(1)} %get-tuple-element.181) | copy-start | bytes 772
  20.2 12.9 %collective-permute-start.1 = (f32[32,4096]{1,0:T(8,128)S(1)}, f32[32,4096]{1,0:T(8,128)S(1)}, u32[]{:S(2)}, u32[]{:S(2)}) collective-permute-start(f32[32,4096]{1,0:T(8,128)S(1)} %pad_maximum_fusion.2), channel_id=1, source_target_pairs={{0,6},{1,7},{2,0},{3,1},{4,2},{5,3},{6,4},{7,5},{8,14},{9,15},{10,... | collective-permute-start | bytes 1572872 | tf_op jit(solution)/shard_map/ppermute | solution.py:22
  34.1 46.6 %collective-permute-start.2 = (f32[64,4096]{1,0:T(8,128)S(1)}, f32[64,4096]{1,0:T(8,128)S(1)}, u32[]{:S(2)}, u32[]{:S(2)}) collective-permute-start(f32[64,4096]{1,0:T(8,128)S(1)} %pad_maximum_fusion.1), channel_id=1, source_target_pairs={{0,4},{1,5},{2,6},{3,7},{4,0},{5,1},{6,2},{7,3},{8,12},{9,13},{10,... | collective-permute-start | bytes 3145736 | tf_op jit(solution)/shard_map/ppermute | solution.py:22
  34.5 56.2 %copy-start.14 = (pred[256]{0:T(512)(128)(4,1)}, pred[256]{0:T(512)(128)(4,1)S(1)}, u32[]{:S(2)}) copy-start(pred[256]{0:T(512)(128)(4,1)S(1)} %compare_and_fusion) | copy-start | bytes 772
  34.6 52.3 %copy-start.11 = (s32[1024]{0:T(1024)}, s32[1024]{0:T(1024)S(1)}, u32[]{:S(2)}) copy-start(s32[1024]{0:T(1024)S(1)} %pad_clamp_fusion) | copy-start | bytes 12292
  166.8 4.3 collective-permute-start.4
  168.1 4.0 collective-permute-start.3
  172.3 21.9 %copy-start.10 = (f32[8]{0:T(128)S(1)}, f32[8]{0:T(128)}, u32[]{:S(2)}) copy-start(f32[8]{0:T(128)} %param.19) | copy-start | bytes 100
  172.5 17.7 %collective-permute-start.5 = (bf16[1152,64]{1,0:T(8,128)(2,1)S(1)}, bf16[1152,64]{1,0:T(8,128)(2,1)S(1)}, u32[]{:S(2)}, u32[]{:S(2)}) collective-permute-start(bf16[1152,64]{1,0:T(8,128)(2,1)S(1)} %get-tuple-element.178), channel_id=1, source_target_pairs={{0,1},{1,2},{2,3},{3,4},{4,5},{5,6},{6,7},{8,9},{9,10},{10,11},{11... | collective-permute-start | bytes 442376 | tf_op jit(solution)/shard_map/ppermute | solution.py:36
  177.6 12.6 %collective-permute-start.6 = (bf16[1152,64]{1,0:T(8,128)(2,1)S(1)}, bf16[1152,64]{1,0:T(8,128)(2,1)S(1)}, u32[]{:S(2)}, u32[]{:S(2)}) collective-permute-start(bf16[1152,64]{1,0:T(8,128)(2,1)S(1)} %get-tuple-element.177), channel_id=1, source_target_pairs={{1,0},{2,1},{3,2},{4,3},{5,4},{6,5},{7,6},{9,8},{10,9},{11,10},{12... | collective-permute-start | bytes 442376 | tf_op jit(solution)/shard_map/ppermute | solution.py:37
  227.3 2.1 copy-start.1
  230.5 5.1 copy-start.2
  241.4 3.2 copy-start
  297.1 2.1 copy-start.1
  300.3 5.1 copy-start.2
  311.2 3.2 copy-start
  367.0 2.1 copy-start.1
  370.1 5.1 copy-start.2
  381.0 3.2 copy-start
  436.8 2.1 copy-start.1
  439.9 5.1 copy-start.2
  450.8 3.2 copy-start
  496.2 2.2 copy-start.3
  496.3 3.5 copy-start.4
  519.7 11.9 %copy-start.9 = (pred[16,16]{1,0:T(8,128)(4,1)S(1)}, pred[16,16]{1,0:T(8,128)(4,1)}, u32[]{:S(2)}) copy-start(pred[16,16]{1,0:T(8,128)(4,1)} %copy-done.8) | copy-start | bytes 772
  542.5 13.1 %copy-start.7 = (pred[16,16]{1,0:T(8,128)(4,1)S(1)}, pred[16,16]{1,0:T(8,128)(4,1)}, u32[]{:S(2)}) copy-start(pred[16,16]{1,0:T(8,128)(4,1)} %copy-done.6) | copy-start | bytes 772
  565.5 7.9 copy-start.13
  578.3 97.1 %all-reduce.3.cloned.1.call-start = ((), (), s32[]{:S(2)}) async-start(), calls=%async_computation.3 | async-start | bytes 262144 | tf_op jit(solution)/shard_map/psum | solution.py:188
  642.3 76.1 %all-gather.2.cloned.1.call-start = ((), (), s32[]{:S(2)}) async-start(), calls=%async_computation.1 | async-start | bytes 1179648 | tf_op jit(solution)/shard_map/all_gather | solution.py:200
  719.9 4.8 copy-start.15
Sparse Core Ops, SparseCore 0:
  578.4 63.8 reduce-scatter.1
  644.6 30.7 all-reduce.2
  678.1 40.2 all-gather.1
